TPU v7x, 128 devices: a whole 4x4x4 slice. The times are simulated.
128 devices in a mesh: row: 8 (over x_lo, z), col: 16 (over y, x_hi, core).
Axes of the slice: x: 4 (x_hi: 2, x_lo: 2; x = x_hi * 2 + x_lo), y: 4, z: 4, core: 2. Of those that a mesh axis runs over, the one named last changes fastest.
Arguments:
- tokens: bfloat16 [1024, 12288], P('col', 'row'), may hold values from -6 to 6
- up_weight: bfloat16 [12288, 24576], P('row', 'col'), may hold values from -0.109375 to 0.109375
- up_mask: int32 [192, 384], P('row', 'col'), may hold values 0 or 1
- down_weight: bfloat16 [24576, 12288], P('col', 'row'), may hold values from -0.078125 to 0.078125
- down_mask: int32 [384, 192], P('col', 'row'), may hold values 0 or 1
- grad_out: bfloat16 [1024, 12288], P('col', 'row'), may hold values from -6 to 6
Outputs:
- out_heads: bfloat16 [96, 1024, 128], P('row', 'col')
- grad_tokens: bfloat16 [1024, 12288], P('col', 'row')
- grad_up: bfloat16 [12288, 24576], P('row', 'col')
- grad_down: bfloat16 [24576, 12288], P('col', 'row')
All inputs are finite; a program needn't handle non-finite values. No bound on the sum of `up_mask` or of `down_mask` on one device may be relied on, other than what follows from the above.
Results may differ from a plain program's by a relative error of at most 0.022.
Values may be sent and summed in bfloat16 or wider, within the bound.
A program may use at most 192 MiB of HBM per device.

v0:
```python
import math

import jax
import jax.numpy as jnp
from jax import lax
from jax.sharding import PartitionSpec as P

BLOCK = 64
HEAD_DIM = 128


def expand(weight, mask):
    rows_in, cols_in = weight.shape
    tiles = weight.reshape(rows_in // BLOCK, BLOCK, cols_in // BLOCK, BLOCK)
    tiles = tiles * mask.astype(weight.dtype)[:, None, :, None]
    return tiles.reshape(rows_in, cols_in)


def activate(value):
    return jax.nn.gelu(value, approximate=True)


def times_transposed(left, right):
    return lax.dot_general(
        left, right, (((1,), (1,)), ((), ())), preferred_element_type=jnp.float32
    )


def over_tokens(left, right):
    return lax.dot_general(
        left, right, (((0,), (0,)), ((), ())), preferred_element_type=jnp.float32
    )


def body(tokens, up_weight, up_mask, down_weight, down_mask, grad_out):
    w_up = expand(up_weight, up_mask)
    w_down = expand(down_weight, down_mask)
    tok_all = lax.all_gather(tokens, "col", axis=0, tiled=True)
    token_count = tok_all.shape[0]
    col_share = token_count // lax.axis_size("col")
    piece = tok_all
    pre_act = lax.psum_scatter(
        jnp.dot(piece, w_up, preferred_element_type=jnp.float32).astype(jnp.bfloat16),
        "row",
        scatter_dimension=0,
        tiled=True,
    ).astype(jnp.float32)
    hidden = activate(pre_act).astype(jnp.bfloat16)
    hidden_all = lax.all_gather(hidden, "row", axis=0, tiled=True)
    piece = hidden_all
    output_rows = lax.psum_scatter(
        jnp.dot(piece, w_down, preferred_element_type=jnp.float32).astype(jnp.bfloat16),
        "col",
        scatter_dimension=0,
        tiled=True,
    )
    out_heads = output_rows.reshape(
        col_share, output_rows.shape[1] // HEAD_DIM, HEAD_DIM
    ).transpose(1, 0, 2)
    cot_all = lax.all_gather(grad_out, "col", axis=0, tiled=True)
    piece = cot_all
    grad_hidden = lax.psum_scatter(
        times_transposed(piece, w_down).astype(jnp.bfloat16), "row", scatter_dimension=0, tiled=True
    ).astype(jnp.float32)
    unused, pull = jax.vjp(activate, pre_act)
    grad_pre = pull(grad_hidden)[0].astype(jnp.bfloat16)
    grad_pre_all = lax.all_gather(grad_pre, "row", axis=0, tiled=True)
    grad_scale = 1.0 / math.sqrt(token_count)
    grad_up = expand(over_tokens(tok_all, grad_pre_all) * grad_scale, up_mask).astype(jnp.bfloat16)
    grad_down = expand(over_tokens(hidden_all, cot_all) * grad_scale, down_mask).astype(
        jnp.bfloat16
    )
    piece = grad_pre_all
    grad_tokens = lax.psum_scatter(
        times_transposed(piece, w_up).astype(jnp.bfloat16), "col", scatter_dimension=0, tiled=True
    )
    return (out_heads, grad_tokens, grad_up, grad_down)


def solution(mesh):
    return jax.shard_map(
        body,
        mesh=mesh,
        in_specs=(
            P("col", "row"),
            P("row", "col"),
            P("row", "col"),
            P("col", "row"),
            P("col", "row"),
            P("col", "row"),
        ),
        out_specs=(P("row", "col", None), P("col", "row"), P("row", "col"), P("col", "row")),
        check_vma=False,
    )
```

profile of v0, /device:TPU:1, one launch (start us, length us, event | category | flops | bytes accessed | tf_op | source)
XLA Modules:
  0.0 488.5 jit_solution(12928435325429374456)
XLA Ops:
  7.2 0.0 all-gather.9.cloned.1.call-start
  7.2 0.7 all-gather.9.cloned.1.call-update
  7.9 0.0 all-gather.5.cloned.1.call-start
  7.9 0.7 all-gather.5.cloned.1.call-update
  8.6 0.0 reduce-scatter.15.cloned.1.call-start
  8.7 0.8 fusion.18
  9.5 4.9 %mul.107 = bf16[24,64,24,64]{3,2,1,0:T(8,128)(2,1)} broadcast(bf16[24,24]{1,0:T(8,128)(2,1)S(1)} %get-tuple-element.19), dimensions={0,2} | broadcast | bytes 4719744 | tf_op jit(solution)/shard_map/mul | solution.py:15
  14.4 13.1 %mul.108 = bf16[1536,1536]{1,0:T(8,128)(2,1)} reshape(bf16[24,64,24,64]{3,2,1,0:T(8,128)(2,1)} %mul.107) | data formatting | bytes 9437184 | tf_op jit(solution)/shard_map/mul | solution.py:15
  27.5 37.0 %all-gather.9.cloned.1.call-done = bf16[1024,1536]{1,0:T(8,128)(2,1)} async-done(((bf16[64,1536]{1,0:T(8,128)(2,1)}), bf16[1024,1536]{1,0:T(8,128)(2,1)}) %all-gather.9.cloned.1.call-update) | async-done | bytes 3145744 | tf_op jit(solution)/shard_map/all_gather | solution.py:60
  64.5 9.5 %fusion.4 = bf16[1024,1536]{0,1:T(8,128)(2,1)S(1)} fusion(bf16[1024,1536]{1,0:T(8,128)(2,1)} %all-gather.9.cloned.1.call-done, bf16[1536,1536]{1,0:T(8,128)(2,1)} %param.9, bf16[1536,1536]{1,0:T(8,128)(2,1)} %mul.108), kind=kOutput, calls=%fused_computation.11 | convolution fusion | flops 4835770368 | bytes 15728640 | tf_op jit(solution)/shard_map/dot_general | solution.py:24
  74.1 2.9 copy.21
  77.0 0.0 reduce-scatter.15.cloned.1.call-update
  77.0 0.2 reduce-scatter.13.cloned.1.call-start
  77.3 4.9 %mul.100 = bf16[24,64,24,64]{3,2,1,0:T(8,128)(2,1)} broadcast(bf16[24,24]{1,0:T(8,128)(2,1)S(1)} %get-tuple-element.21), dimensions={0,2} | broadcast | bytes 4719744 | tf_op jit(solution)/shard_map/mul | solution.py:15
  82.2 13.0 %mul.101 = bf16[1536,1536]{1,0:T(8,128)(2,1)} reshape(bf16[24,64,24,64]{3,2,1,0:T(8,128)(2,1)} %mul.100) | data formatting | bytes 9437184 | tf_op jit(solution)/shard_map/mul | solution.py:15
  95.3 7.6 %mul.102 = bf16[1536,1536]{1,0:T(8,128)(2,1)} multiply(bf16[1536,1536]{1,0:T(8,128)(2,1)} %param.7, bf16[1536,1536]{1,0:T(8,128)(2,1)} %mul.101) | non-fusion elementwise | flops 2359296 | bytes 14155776 | tf_op jit(solution)/shard_map/mul | solution.py:15
  102.9 13.4 %all-gather.5.cloned.1.call-done = bf16[1024,1536]{1,0:T(8,128)(2,1)} async-done(((bf16[64,1536]{1,0:T(8,128)(2,1)}), bf16[1024,1536]{1,0:T(8,128)(2,1)}) %all-gather.5.cloned.1.call-update) | async-done | bytes 3145744 | tf_op jit(solution)/shard_map/all_gather | solution.py:38
  116.3 8.2 %fusion.3 = bf16[1024,1536]{0,1:T(8,128)(2,1)S(1)} fusion(bf16[1536,1536]{1,0:T(8,128)(2,1)} %mul.102, bf16[1024,1536]{1,0:T(8,128)(2,1)} %all-gather.5.cloned.1.call-done), kind=kOutput, calls=%fused_computation.10 | convolution fusion | flops 4833411072 | bytes 11010048 | tf_op jit(solution)/shard_map/dot_general | solution.py:43
  124.5 3.0 copy.19
  127.4 0.0 reduce-scatter.13.cloned.1.call-update
  127.5 0.0 all-gather.7.cloned.1.call-start
  127.5 32.3 %reduce-scatter.15.cloned.1.call-done = bf16[128,1536]{1,0:T(8,128)(2,1)} async-done(((bf16[1024,1536]{1,0:T(8,128)(2,1)}), bf16[128,1536]{1,0:T(8,128)(2,1)}) %reduce-scatter.15.cloned.1.call-update) | async-done | bytes 393232
  159.8 1.2 copy.22
  161.0 47.1 %reduce-scatter.13.cloned.1.call-done = bf16[128,1536]{1,0:T(8,128)(2,1)} async-done(((bf16[1024,1536]{1,0:T(8,128)(2,1)}), bf16[128,1536]{1,0:T(8,128)(2,1)}) %reduce-scatter.13.cloned.1.call-update) | async-done | bytes 393232
  208.1 1.2 copy.20
  209.4 1.5 fusion.10
  210.9 0.0 all-gather.7.cloned.1.call-update
  210.9 0.0 all-gather.11.cloned.1.call-start
  211.0 0.5 all-gather.11.cloned.1.call-update
  211.5 0.0 reduce-scatter.9.cloned.1.call-start
  211.5 51.2 %all-gather.7.cloned.1.call-done = bf16[1024,1536]{0,1:T(8,128)(2,1)} async-done(((bf16[128,1536]{0,1:T(8,128)(2,1)}), bf16[1024,1536]{0,1:T(8,128)(2,1)}) %all-gather.7.cloned.1.call-update) | async-done | bytes 3145744 | tf_op jit(solution)/shard_map/all_gather | solution.py:49
  262.7 10.7 %convolution_convert_fusion.2 = bf16[1024,1536]{1,0:T(8,128)(2,1)} fusion(bf16[1024,1536]{0,1:T(8,128)(2,1)} %all-gather.7.cloned.1.call-done, bf16[1536,1536]{1,0:T(8,128)(2,1)} %param.9, bf16[1536,1536]{1,0:T(8,128)(2,1)} %mul.108), kind=kOutput, calls=%fused_computation.8 | convolution fusion | flops 4835770368 | bytes 15728640 | tf_op jit(solution)/shard_map/dot_general | solution.py:52
  273.4 0.0 reduce-scatter.9.cloned.1.call-update
  273.4 0.3 reduce-scatter.11.cloned.1.call-start
  273.7 45.0 %all-gather.11.cloned.1.call-done = bf16[1024,1536]{0,1:T(8,128)(2,1)} async-done(((bf16[128,1536]{0,1:T(8,128)(2,1)}), bf16[1024,1536]{0,1:T(8,128)(2,1)}) %all-gather.11.cloned.1.call-update) | async-done | bytes 3145744 | tf_op jit(solution)/shard_map/all_gather | solution.py:67
  318.7 9.3 %convolution_convert_fusion = bf16[1024,1536]{1,0:T(8,128)(2,1)} fusion(bf16[1024,1536]{0,1:T(8,128)(2,1)} %all-gather.11.cloned.1.call-done, bf16[1536,1536]{1,0:T(8,128)(2,1)} %mul.102), kind=kOutput, calls=%fused_computation.6 | convolution fusion | flops 4833411072 | bytes 11010048 | tf_op jit(solution)/shard_map/dot_general | solution.py:24
  328.0 0.0 reduce-scatter.11.cloned.1.call-update
  328.0 0.1 copy.16
  328.0 7.8 %mul.127 = f32[24,64,24,64]{3,2,1,0:T(8,128)} broadcast(f32[24,24]{1,0:T(8,128)S(1)} %get-tuple-element.18), dimensions={0,2} | broadcast | bytes 9439488 | tf_op jit(solution)/shard_map/mul | solution.py:15
  335.8 16.7 %mul.128 = f32[1536,1536]{1,0:T(8,128)} reshape(f32[24,64,24,64]{3,2,1,0:T(8,128)} %mul.127) | data formatting | bytes 18874368 | tf_op jit(solution)/shard_map/mul | solution.py:15
  352.5 7.7 %mul.123 = f32[24,64,24,64]{1,0,3,2:T(8,128)} broadcast(f32[24,24]{0,1:T(8,128)S(1)} %copy.16), dimensions={0,2} | broadcast | bytes 9439488 | tf_op jit(solution)/shard_map/mul | solution.py:15
  360.2 16.7 %mul.124 = f32[1536,1536]{0,1:T(8,128)} reshape(f32[24,64,24,64]{1,0,3,2:T(8,128)} %mul.123) | data formatting | bytes 18874368 | tf_op jit(solution)/shard_map/mul | solution.py:15
  376.9 10.1 %fusion.1 = bf16[1536,1536]{0,1:T(8,128)(2,1)} fusion(f32[1536,1536]{0,1:T(8,128)} %mul.124, bf16[1024,1536]{0,1:T(8,128)(2,1)} %all-gather.11.cloned.1.call-done, bf16[1024,1536]{1,0:T(8,128)(2,1)S(1)} %copy-done.2), kind=kOutput, calls=%fused_computation.4 | convolution fusion | flops 4838916096 | bytes 20447232 | tf_op jit(solution)/shard_map/dot_general | solution.py:30
  387.0 6.8 %copy.18 = bf16[1536,1536]{1,0:T(8,128)(2,1)} copy(bf16[1536,1536]{0,1:T(8,128)(2,1)} %fusion.1) | data formatting | bytes 9437184
  393.8 10.1 %fusion.2 = bf16[1536,1536]{1,0:T(8,128)(2,1)} fusion(f32[1536,1536]{1,0:T(8,128)} %mul.128, bf16[1024,1536]{0,1:T(8,128)(2,1)} %all-gather.7.cloned.1.call-done, bf16[1024,1536]{1,0:T(8,128)(2,1)S(1)} %copy-done.1), kind=kOutput, calls=%fused_computation.5 | convolution fusion | flops 4838916096 | bytes 20447232 | tf_op jit(solution)/shard_map/dot_general | solution.py:30
  403.8 1.1 reshape.27
  404.9 0.7 copy.17
  405.7 76.0 %reduce-scatter.11.cloned.1.call-done = bf16[64,1536]{1,0:T(8,128)(2,1)} async-done(((bf16[1024,1536]{1,0:T(8,128)(2,1)}), bf16[64,1536]{1,0:T(8,128)(2,1)}) %reduce-scatter.11.cloned.1.call-update) | async-done | bytes 196624 | tf_op jit(solution)/shard_map/reduce_scatter | solution.py:74
  (8 shorter events, 0.0 us)
Async XLA Ops:
  7.2 57.3 %all-gather.9.cloned.1.call-start = ((), (), s32[]{:S(2)}) async-start(), calls=%async_computation.7 | async-start | bytes 3342336 | tf_op jit(solution)/shard_map/all_gather | solution.py:60
  7.9 108.4 %all-gather.5.cloned.1.call-start = ((), (), s32[]{:S(2)}) async-start(), calls=%async_computation.4 | async-start | bytes 3342336 | tf_op jit(solution)/shard_map/all_gather | solution.py:38
  8.6 151.2 %reduce-scatter.15.cloned.1.call-start = ((), (), s32[]{:S(2)}) async-start(), calls=%async_computation.11 | async-start | bytes 3538944
  74.1 3.2 copy-start
  77.0 131.1 %reduce-scatter.13.cloned.1.call-start = ((), (), s32[]{:S(2)}) async-start(), calls=%async_computation.10 | async-start | bytes 3538944
  127.5 135.3 %all-gather.7.cloned.1.call-start = ((), (), s32[]{:S(2)}) async-start(), calls=%async_computation.5 | async-start | bytes 3538944 | tf_op jit(solution)/shard_map/all_gather | solution.py:49
  210.9 107.7 %all-gather.11.cloned.1.call-start = ((), (), s32[]{:S(2)}) async-start(), calls=%async_computation.8 | async-start | bytes 3538944 | tf_op jit(solution)/shard_map/all_gather | solution.py:67
  211.5 192.3 %reduce-scatter.9.cloned.1.call-start = ((), (), s32[]{:S(2)}) async-start(), calls=%async_computation.6 | async-start | bytes 3342336 | tf_op jit(solution)/shard_map/reduce_scatter | solution.py:51
  273.4 208.2 %reduce-scatter.11.cloned.1.call-start = ((), (), s32[]{:S(2)}) async-start(), calls=%async_computation.9 | async-start | bytes 3342336 | tf_op jit(solution)/shard_map/reduce_scatter | solution.py:74
  360.2 16.7 %copy-start.2 = (bf16[1024,1536]{1,0:T(8,128)(2,1)S(1)}, bf16[1024,1536]{1,0:T(8,128)(2,1)}, u32[]{:S(2)}) copy-start(bf16[1024,1536]{1,0:T(8,128)(2,1)} %all-gather.5.cloned.1.call-done) | copy-start | bytes 9437188
  387.0 6.8 %copy-start.1 = (bf16[1024,1536]{1,0:T(8,128)(2,1)S(1)}, bf16[1024,1536]{1,0:T(8,128)(2,1)}, u32[]{:S(2)}) copy-start(bf16[1024,1536]{1,0:T(8,128)(2,1)} %all-gather.9.cloned.1.call-done) | copy-start | bytes 9437188
Sparse Core Ops, SparseCore 0:
  10.4 54.0 all-gather.8
  67.0 49.2 all-gather.4
  118.7 41.0 reduce-scatter.14
  162.1 46.0 reduce-scatter.12
  211.0 51.6 all-gather.6
  264.1 54.4 all-gather.10
  322.7 80.0 reduce-scatter.8
  407.4 74.1 reduce-scatter.10
where the time goes:
time: 491 us; the launch traced here: 488 us
  waiting for transfers between devices  304 us (62%)
  local copies, waits for them, and re-layouts  102 us (21%)
  matrix products  57.8 us (12%)
  between operations  14.2 us (3%)
  other arithmetic  9.97 us (2%)
    mul x8, local copies, waits for them, and re-layouts, expand(): tiles = tiles * mask.astype(weight.dtype)[:, None, :, None]  84.9 us
    unnamed x10, waiting for transfers between devices  81.4 us
    reduce_scatter x1, waiting for transfers between devices, body(): lax.psum_scatter(times_transposed(piece, w_up).astype(jnp.bfloat16), 'col...  76 us
    all_gather x1, waiting for transfers between devices, body(): hidden_all = lax.all_gather(hidden, 'row', axis=0, tiled=True)  51.2 us
    all_gather x1, waiting for transfers between devices, body(): grad_pre_all = lax.all_gather(grad_pre, 'row', axis=0, tiled=True)  45 us
    all_gather x1, waiting for transfers between devices, body(): cot_all = lax.all_gather(grad_out, 'col', axis=0, tiled=True)  37 us
    dot_general x2, matrix products, over_tokens(): lax.dot_general(left, right, (((0,), (0,)), ((), ())), preferred_element_...  20.1 us
    dot_general x2, matrix products, times_transposed(): lax.dot_general(left, right, (((1,), (1,)), ((), ())), preferred_element_...  18.8 us
  transfers between devices with their start and end apart: 8, of which 7 were waited for; matrix products, arithmetic and copies ran while one was open for 34% of the time, Pallas kernels for 0%

commit v1 on v0

v1 whole, which is shorter than its diff:
```python
import functools
import math

import jax
import jax.numpy as jnp
from jax import lax
from jax.experimental import pallas as pl
from jax.experimental.pallas import tpu as pltpu
from jax.sharding import PartitionSpec as P

BLOCK = 64
HEAD_DIM = 128
CHUNKS = 4
TILE = 256
MESH = pl.DeviceIdType.MESH
F32 = jnp.float32
BF16 = jnp.bfloat16

AG_XH, AG_Y, AG_CORE = 0, 1, 4
A_X, A_Z, B_Z, B_X = 5, 6, 9, 12
C_X, C_Z, D_Z, D_X = 13, 14, 17, 20
R_CORE, R_Y, R_XH = 21, 22, 25
MESSAGES = 26


def dot_nn(left, right):
    return jnp.dot(left, right, preferred_element_type=F32)


def dot_nt(left, right):
    return lax.dot_general(left, right, (((1,), (1,)), ((), ())), preferred_element_type=F32)


def dot_tn(left, right):
    return lax.dot_general(left, right, (((0,), (0,)), ((), ())), preferred_element_type=F32)


def tile_at(index):
    return pl.ds(pl.multiple_of(index * TILE, TILE), TILE)


def kernel(
    tok, wup, mup, wdn, mdn, cot,
    oh, gt, gu, gd,
    tc, wu, wd, m2u, m2d, pa, pb, ra, rb, sb, sbo, r3a, r3b, hid, gra, out, r7a, r7b, s8, r7c,
    ss, rs, ls,
):
    width = tok.shape[1]
    tokens = tc.shape[0]
    chunk = tokens // CHUNKS
    piece = tok.shape[0] // CHUNKS
    tiles = width // TILE
    grad_scale = 1.0 / math.sqrt(tokens)

    row, col = lax.axis_index("row"), lax.axis_index("col")
    xl, z = row // 4, row % 4
    y, xh, k = col // 4, (col // 2) % 2, col % 2

    def device(xl=xl, z=z, y=y, xh=xh, k=k):
        return (xl * 4 + z, y * 4 + xh * 2 + k)

    z_to = [(z + d) % 4 for d in (1, 2, 3)]
    z_from = [(z + 4 - d) % 4 for d in (1, 2, 3)]
    y_to = [(y + d) % 4 for d in (1, 2, 3)]
    y_from = [(y + 4 - d) % 4 for d in (1, 2, 3)]
    x_dev, xh_dev, core_dev = device(xl=1 - xl), device(xh=1 - xh), device(k=1 - k)
    z_dev = [device(z=v) for v in z_to]
    y_dev = [device(y=v) for v in y_to]

    def rows_of(j, k_, y_, xh_, pieces):
        at = j * chunk + k_ * (chunk // 2) + y_ * (2 * piece) + xh_ * piece
        return pl.ds(pl.multiple_of(at, piece), pieces * piece)

    pending = []

    def send(j, i, src, dst, dev):
        copy = pltpu.make_async_remote_copy(
            src_ref=src, dst_ref=dst, send_sem=ss.at[j, i], recv_sem=rs.at[j, i],
            device_id=dev, device_id_type=MESH,
        )
        copy.start()
        pending.append(copy)

    def arrived(j, i, here, dev):
        pltpu.make_async_remote_copy(
            src_ref=here, dst_ref=here, send_sem=ss.at[j, i], recv_sem=rs.at[j, i],
            device_id=dev, device_id_type=MESH,
        ).wait_recv()

    own = []
    for j in range(CHUNKS):
        there = rows_of(j, k, y, xh, 1)
        here = pl.ds(j * piece, piece)
        pair = (
            pltpu.make_async_copy(tok.at[here], tc.at[there, pl.ds(0, width)], ls.at[2 * j]),
            pltpu.make_async_copy(cot.at[here], tc.at[there, pl.ds(width, width)], ls.at[2 * j + 1]),
        )
        for copy in pair:
            copy.start()
        own.append(pair)
    load_up = pltpu.make_async_copy(wup, wu, ls.at[2 * CHUNKS])
    load_dn = pltpu.make_async_copy(wdn, wd, ls.at[2 * CHUNKS + 1])
    load_up.start()
    load_dn.start()

    barrier = pltpu.get_barrier_semaphore()
    for dev in [x_dev, xh_dev, core_dev] + z_dev + y_dev:
        pl.semaphore_signal(barrier, inc=1, device_id=dev, device_id_type=MESH)
    pl.semaphore_wait(barrier, 9)

    def ag_x(j):
        for copy in own[j]:
            copy.wait()
        at = tc.at[rows_of(j, k, y, xh, 1)]
        send(j, AG_XH, at, at, xh_dev)

    def ag_y(j):
        arrived(j, AG_XH, tc.at[rows_of(j, k, y, 1 - xh, 1)], xh_dev)
        at = tc.at[rows_of(j, k, y, 0, 2)]
        for d in range(3):
            send(j, AG_Y + d, at, at, y_dev[d])

    def ag_core(j):
        for d in range(3):
            arrived(j, AG_Y + d, tc.at[rows_of(j, k, y_from[d], 0, 2)], y_dev[d])
        at = tc.at[rows_of(j, k, 0, 0, 8)]
        send(j, AG_CORE, at, at, core_dev)

    def up(j):
        arrived(j, AG_CORE, tc.at[rows_of(j, 1 - k, 0, 0, 8)], core_dev)
        rows = pl.ds(j * chunk, chunk)

        @pl.loop(0, tiles)
        def _(n):
            value = dot_nn(tc[rows, pl.ds(0, width)], wu[:, tile_at(n)]).astype(BF16)
            pa[j, :, :, :, tile_at(n)] = value.reshape(2, 4, chunk // 8, TILE)

        send(j, A_X, pa.at[j, 1 - xl], ra.at[j], x_dev)

        @pl.loop(0, tiles)
        def _(n):
            value = dot_nt(tc[rows, pl.ds(width, width)], wd[tile_at(n), :]).astype(BF16)
            pb[j, :, :, :, tile_at(n)] = value.reshape(2, 4, chunk // 8, TILE)

        for d in range(3):
            send(j, A_Z + d, pb.at[j, :, z_to[d]], rb.at[j, d], z_dev[d])

    def sum_a(j):
        arrived(j, A_X, ra.at[j], x_dev)

        @pl.loop(0, 4)
        def _(v):
            pa[j, xl, v] = (pa[j, xl, v].astype(F32) + ra[j, v].astype(F32)).astype(BF16)

        for d in range(3):
            send(j, B_Z + d, pa.at[j, xl, z_to[d]], r3a.at[j, d], z_dev[d])
        for d in range(3):
            arrived(j, A_Z + d, rb.at[j, d], z_dev[d])

        def total(v):
            value = pb[j, v, z].astype(F32)
            for d in range(3):
                value = value + rb[j, d, v].astype(F32)
            return value

        sb[j] = total(1 - xl).astype(BF16)
        send(j, B_X, sb.at[j], r3b.at[j], x_dev)
        sbo[j] = total(xl)

    def sum_b(j):
        for d in range(3):
            arrived(j, B_Z + d, r3a.at[j, d], z_dev[d])
        arrived(j, B_X, r3b.at[j], x_dev)
        pre = pa[j, xl, z].astype(F32)
        for d in range(3):
            pre = pre + r3a[j, d].astype(F32)
        back = sbo[j] + r3b[j].astype(F32)
        root = 0.7978845608028654
        square = pre * pre
        bend = jnp.tanh(root * (pre + 0.044715 * (square * pre)))
        half = 0.5 * (1.0 + bend)
        slope = half + 0.5 * pre * (1.0 - bend * bend) * (root * (1.0 + 3 * 0.044715 * square))
        hid[j, xl, z] = (pre * half).astype(BF16)
        gra[j, xl, z] = (back * slope).astype(BF16)
        for d in range(3):
            send(j, C_Z + d, gra.at[j, xl, z], gra.at[j, xl, z], z_dev[d])
        send(j, C_X, hid.at[j, xl, z], hid.at[j, xl, z], x_dev)

    def spread(j):
        arrived(j, C_X, hid.at[j, 1 - xl, z], x_dev)
        for d in range(3):
            send(j, D_Z + d, hid.at[j, :, z], hid.at[j, :, z], z_dev[d])
        for d in range(3):
            arrived(j, C_Z + d, gra.at[j, xl, z_from[d]], z_dev[d])
        send(j, D_X, gra.at[j, xl], gra.at[j, xl], x_dev)

    def down(j):
        for d in range(3):
            arrived(j, D_Z + d, hid.at[j, :, z_from[d]], z_dev[d])

        @pl.loop(0, tiles)
        def _(n):
            value = dot_nn(hid[j].reshape(chunk, width), wd[:, tile_at(n)]).astype(BF16)
            out[j, :, :, :, tile_at(n)] = value.reshape(2, 4, 2 * piece, TILE)

        arrived(j, D_X, gra.at[j, 1 - xl], x_dev)

        @pl.loop(0, tiles)
        def _(n):
            value = dot_nt(gra[j].reshape(chunk, width), wu[tile_at(n), :]).astype(BF16)
            out[j, :, :, :, tile_at(n + tiles)] = value.reshape(2, 4, 2 * piece, TILE)

        send(j, R_CORE, out.at[j, 1 - k], r7a.at[j], core_dev)

    def rs_core(j):
        arrived(j, R_CORE, r7a.at[j], core_dev)

        @pl.loop(0, 4)
        def _(v):
            out[j, k, v] = (out[j, k, v].astype(F32) + r7a[j, v].astype(F32)).astype(BF16)

        for d in range(3):
            send(j, R_Y + d, out.at[j, k, y_to[d]], r7b.at[j, d], y_dev[d])

    def rs_y(j):
        for d in range(3):
            arrived(j, R_Y + d, r7b.at[j, d], y_dev[d])
        value = out[j, k, y].astype(F32)
        for d in range(3):
            value = value + r7b[j, d].astype(F32)
        s8[j] = value.astype(BF16).reshape(2, piece, 2 * width)
        send(j, R_XH, s8.at[j, 1 - xh], r7c.at[j], xh_dev)

    def rs_x(j):
        arrived(j, R_XH, r7c.at[j], xh_dev)
        value = (s8[j, xh].astype(F32) + r7c[j].astype(F32)).astype(BF16)
        here = pl.ds(j * piece, piece)
        for head in range(width // HEAD_DIM):
            oh[head, here, :] = value[:, head * HEAD_DIM:(head + 1) * HEAD_DIM]
        gt[here, :] = value[:, width:]

    def weight_grad(left, right, mask, place, result, sem):
        @pl.loop(0, tiles)
        def _(m):
            @pl.loop(0, tiles)
            def _(n):
                value = dot_tn(left(tile_at(m)), right(tile_at(n))) * grad_scale
                for b in range(TILE // BLOCK):
                    keep = mask[pl.ds(m * (TILE // BLOCK) + b, 1), tile_at(n)]
                    part = value[b * BLOCK:(b + 1) * BLOCK] * keep
                    at = pl.ds(pl.multiple_of(m * TILE + b * BLOCK, BLOCK), BLOCK)
                    place[at, tile_at(n)] = part.astype(BF16)

        copy = pltpu.make_async_copy(place, result, sem)
        copy.start()
        return copy

    def grad_up():
        return weight_grad(
            lambda t: tc[:, t],
            lambda t: gra[:, :, :, :, t].reshape(tokens, TILE),
            m2u, wu, gu, ls.at[2 * CHUNKS + 2],
        )

    def grad_down():
        return weight_grad(
            lambda t: hid[:, :, :, :, t].reshape(tokens, TILE),
            lambda t: tc[:, pl.ds(pl.multiple_of(t.start + width, TILE), TILE)],
            m2d, wd, gd, ls.at[2 * CHUNKS + 3],
        )

    for j in range(CHUNKS):
        ag_x(j)
    for j in range(CHUNKS):
        ag_y(j)

    blocks = width // BLOCK
    at = lax.broadcasted_iota(jnp.int32, (blocks, width), 1)
    first = lax.broadcasted_iota(jnp.int32, (blocks, width), 0) * BLOCK
    repeat = jnp.where((at >= first) & (at < first + BLOCK), 1.0, 0.0).astype(F32)
    for mask, wide, weight, load in ((mup, m2u, wu, load_up), (mdn, m2d, wd, load_dn)):
        wide[...] = dot_nn(mask[...].astype(F32), repeat)
        load.wait()

        @pl.loop(0, blocks)
        def _(b):
            rows = pl.ds(pl.multiple_of(b * BLOCK, BLOCK), BLOCK)
            weight[rows, :] = (weight[rows, :].astype(F32) * wide[pl.ds(b, 1), :]).astype(BF16)

    for j in (0, 1):
        ag_core(j)
        up(j)
    for step in (sum_a, sum_b):
        for j in (0, 1):
            step(j)
    for j in (2, 3):
        ag_core(j)
    for j in (0, 1):
        spread(j)
    for j in (2, 3):
        up(j)
    for j in (0, 1):
        down(j)
    for j in (2, 3):
        sum_a(j)
    for j in (0, 1):
        rs_core(j)
    for j in (2, 3):
        sum_b(j)
    for j in (0, 1):
        rs_y(j)
    for j in (2, 3):
        spread(j)
    for j in (0, 1):
        rs_x(j)
    down(2)
    rs_core(2)
    down(3)
    stores = [grad_up()]
    rs_core(3)
    rs_y(2)
    stores.append(grad_down())
    rs_y(3)
    rs_x(2)
    rs_x(3)
    for copy in pending:
        copy.wait_send()
    for copy in stores:
        copy.wait()


def body(tokens, up_weight, up_mask, down_weight, down_mask, grad_out):
    share, width = tokens.shape
    total = share * lax.axis_size("col")
    part = total // CHUNKS // 8
    piece = share // CHUNKS
    blocks = width // BLOCK
    c = CHUNKS
    hbm = pl.BlockSpec(memory_space=pl.ANY)
    vmem = pl.BlockSpec(memory_space=pltpu.VMEM)
    return pl.pallas_call(
        kernel,
        out_shape=(
            jax.ShapeDtypeStruct((width // HEAD_DIM, share, HEAD_DIM), BF16),
            jax.ShapeDtypeStruct((share, width), BF16),
            jax.ShapeDtypeStruct(up_weight.shape, BF16),
            jax.ShapeDtypeStruct(down_weight.shape, BF16),
        ),
        in_specs=[hbm, hbm, vmem, hbm, vmem, hbm],
        out_specs=(vmem, vmem, hbm, hbm),
        scratch_shapes=[
            pltpu.VMEM((total, 2 * width), BF16),
            pltpu.VMEM(up_weight.shape, BF16),
            pltpu.VMEM(down_weight.shape, BF16),
            pltpu.VMEM((blocks, width), F32),
            pltpu.VMEM((blocks, width), F32),
            pltpu.VMEM((c, 2, 4, part, width), BF16),
            pltpu.VMEM((c, 2, 4, part, width), BF16),
            pltpu.VMEM((c, 4, part, width), BF16),
            pltpu.VMEM((c, 3, 2, part, width), BF16),
            pltpu.VMEM((c, part, width), BF16),
            pltpu.VMEM((c, part, width), F32),
            pltpu.VMEM((c, 3, part, width), BF16),
            pltpu.VMEM((c, part, width), BF16),
            pltpu.VMEM((c, 2, 4, part, width), BF16),
            pltpu.VMEM((c, 2, 4, part, width), BF16),
            pltpu.VMEM((c, 2, 4, 2 * piece, 2 * width), BF16),
            pltpu.VMEM((c, 4, 2 * piece, 2 * width), BF16),
            pltpu.VMEM((c, 3, 2 * piece, 2 * width), BF16),
            pltpu.VMEM((c, 2, piece, 2 * width), BF16),
            pltpu.VMEM((c, piece, 2 * width), BF16),
            pltpu.SemaphoreType.DMA((c, MESSAGES)),
            pltpu.SemaphoreType.DMA((c, MESSAGES)),
            pltpu.SemaphoreType.DMA((2 * c + 4,)),
        ],
        compiler_params=pltpu.CompilerParams(
            collective_id=0, has_side_effects=True, vmem_limit_bytes=67043328
        ),
        name="layer",
    )(tokens, up_weight, up_mask, down_weight, down_mask, grad_out)


def solution(mesh):
    return jax.shard_map(
        body,
        mesh=mesh,
        in_specs=(
            P("col", "row"),
            P("row", "col"),
            P("row", "col"),
            P("col", "row"),
            P("col", "row"),
            P("col", "row"),
        ),
        out_specs=(P("row", "col", None), P("col", "row"), P("row", "col"), P("col", "row")),
        check_vma=False,
    )
```

time: 491 us -> 190 us (0.39)
  waiting for transfers between devices: 304 us -> 0 us
  Pallas kernels: 0 us -> 178 us
  local copies, waits for them, and re-layouts: 102 us -> 10.5 us
  matrix products: 57.8 us -> 0 us
  between operations: 14.2 us -> 0.64 us
  other arithmetic: 9.97 us -> 0.01 us
    pallas_call x0 -> x1, Pallas kernels: none -> 178 us  [body(): pl.pallas_call(kernel, out_shape=(jax.ShapeDtypeStruct((width // HEAD_DIM...]
    all_gather x4 -> x0, waiting for transfers between devices: 147 us -> none  [the longest x1 51.2 us: body(): hidden_all = lax.all_gather(hidden, 'row', axis=0, tiled=True)]
    mul x8 -> x0, local copies, waits for them, and re-layouts: 84.9 us -> none  [expand(): tiles = tiles * mask.astype(weight.dtype)[:, None, :, None]]
    unnamed x10 -> x0, waiting for transfers between devices: 81.4 us -> none
    reduce_scatter x2 -> x0, waiting for transfers between devices: 76 us -> none  [the longest x1 76 us: body(): lax.psum_scatter(times_transposed(piece, w_up).astype(jnp.bfloat16), 'col...]
    dot_general x6 -> x0, matrix products: 57.8 us -> none  [the longest x2 20.1 us: over_tokens(): lax.dot_general(left, right, (((0,), (0,)), ((), ())), preferred_element_...]
    mul x1 -> x0, other arithmetic: 7.64 us -> none  [expand(): tiles = tiles * mask.astype(weight.dtype)[:, None, :, None]]
    unnamed x12 -> x8, local copies, waits for them, and re-layouts: 15.8 us -> 10.5 us
  transfers between devices with their start and end apart: 8 -> 0, of which waited for: 7 -> 0; matrix products, arithmetic and copies ran while one was open for 34% -> 0% of each run, Pallas kernels for 0% -> 0%
where the time goes in v1:
time: 190 us; the launch traced here: 189 us
  Pallas kernels  178 us (94%)
  local copies, waits for them, and re-layouts  10.5 us (6%)
    pallas_call x1, Pallas kernels, body(): pl.pallas_call(kernel, out_shape=(jax.ShapeDtypeStruct((width // HEAD_DIM...  178 us
    unnamed x8, local copies, waits for them, and re-layouts  10.5 us

profile of v1, /device:TPU:1, one launch (start us, length us, event | category | flops | bytes accessed | tf_op | source)
XLA Modules:
  0.0 189.1 jit_solution(14498417836963818719)
XLA Ops:
  0.6 178.0 %layer.1 = (bf16[12,64,128]{2,1,0:T(8,128)(2,1)}, bf16[64,1536]{1,0:T(8,128)(2,1)}, bf16[1536,1536]{1,0:T(8,128)(2,1)}, bf16[1536,1536]{1,0:T(8,128)(2,1)}) custom-call(bf16[64,1536]{1,0:T(8,128)(2,1)} %tok.1, bf16[1536,1536]{1,0:T(8,128)(2,1)} %wup.1, s32[24,24]{1,0:T(8,128)} %mup.1, bf16[1536,1536]{1,0:T(8,128)(2,1)} %wdn.1, s32[24,24]{1,0:T(8,128)} %mdn.1, ...), custom_call_target="tpu_custom_call" | custom-call | tf_op jit(solution)/shard_map/layer/pallas_call | solution.py:341
  178.7 1.6 copy.14
  180.3 0.0 slice-start
  180.3 1.8 copy.15
  182.1 0.0 slice-start.1
  182.1 4.9 %copy.16 = bf16[1536,1536]{1,0:T(8,128)(2,1)} copy(bf16[1536,1536]{1,0:T(8,128)(2,1)} %get-tuple-element.10) | data formatting | bytes 9437184
  187.0 0.0 slice-done
  187.0 0.0 slice-done.1
  187.0 2.2 %copy.17 = bf16[1536,1536]{1,0:T(8,128)(2,1)} copy(bf16[1536,1536]{1,0:T(8,128)(2,1)S(1)} %bitcast.1) | data formatting | bytes 9437184
  (1 shorter events, 0.0 us)
Async XLA Ops:
  180.3 6.7 %slice-start = ((s8[4718592]{0:T(1024)(128)(4,1)}), s8[4194304]{0:T(1024)(128)(4,1)S(1)}, s32[]{:S(2)}) async-start(s8[4718592]{0:T(1024)(128)(4,1)} %bitcast), calls=%async_computation | async-start | bytes 8388608
  182.1 4.9 %slice-start.1 = ((s8[4718592]{0:T(1024)(128)(4,1)}), s8[524288]{0:T(1024)(128)(4,1)S(1)}, s32[]{:S(2)}) async-start(s8[4718592]{0:T(1024)(128)(4,1)} %bitcast), calls=%async_computation.1 | async-start | bytes 1048576

commit v2 on v1

v2 whole, which is shorter than its diff:
```python
import functools
import math

import jax
import jax.numpy as jnp
from jax import lax
from jax.experimental import pallas as pl
from jax.experimental.pallas import tpu as pltpu
from jax.sharding import PartitionSpec as P

BLOCK = 64
HEAD_DIM = 128
CHUNKS = 4
TILE = 256
WIDE = 768
GRAD_WIDE = 768
MESH = pl.DeviceIdType.MESH
F32 = jnp.float32
BF16 = jnp.bfloat16

AG_XH, AG_Y, AG_CORE = (0, 5), (1, 6), (4, 9)
R_CORE, R_Y, R_XH = (10, 15), (11, 16), (14, 19)
A_X, A_Z, B_Z, B_X = 20, 21, 24, 27
C_X, C_Z, D_Z, D_X = 28, 29, 32, 35
MESSAGES = 36
FWD, BWD = 0, 1


def dot_nn(left, right):
    return jnp.dot(left, right, preferred_element_type=F32)


def dot_nt(left, right):
    return lax.dot_general(left, right, (((1,), (1,)), ((), ())), preferred_element_type=F32)


def tile_at(index, tile=TILE):
    return pl.ds(pl.multiple_of(index * tile, tile), tile)


def kernel(
    tok, wup, mup, wdn, mdn, cot,
    oh, gt, gu, gd,
    tall, call, tturn, hturn, wu, wd, m2u, m2d, pa, pb, ra, rb, sb, sbo, r3a, r3b, hid, gra,
    outf, outb, r7f, r7b, ryf, ryb, s8f, s8b, rxf, rxb,
    ss, rs, ls,
):
    width = tok.shape[1]
    tokens = tall.shape[0]
    chunk = tokens // CHUNKS
    piece = tok.shape[0] // CHUNKS
    tiles = width // TILE
    grad_scale = 1.0 / math.sqrt(tokens)
    every = (tall, call)
    out, r_core, r_y, s_x, r_x = (outf, outb), (r7f, r7b), (ryf, ryb), (s8f, s8b), (rxf, rxb)

    row, col = lax.axis_index("row"), lax.axis_index("col")
    xl, z = row // 4, row % 4
    y, xh, k = col // 4, (col // 2) % 2, col % 2

    def device(xl=xl, z=z, y=y, xh=xh, k=k):
        return (xl * 4 + z, y * 4 + xh * 2 + k)

    z_to = [(z + d) % 4 for d in (1, 2, 3)]
    z_from = [(z + 4 - d) % 4 for d in (1, 2, 3)]
    y_to = [(y + d) % 4 for d in (1, 2, 3)]
    y_from = [(y + 4 - d) % 4 for d in (1, 2, 3)]
    x_dev, xh_dev, core_dev = device(xl=1 - xl), device(xh=1 - xh), device(k=1 - k)
    z_dev = [device(z=v) for v in z_to]
    y_dev = [device(y=v) for v in y_to]

    def rows_of(j, k_, y_, xh_, pieces):
        at = j * chunk + k_ * (chunk // 2) + y_ * (2 * piece) + xh_ * piece
        return pl.ds(pl.multiple_of(at, piece), pieces * piece)

    pending = []

    def send(j, i, src, dst, dev):
        copy = pltpu.make_async_remote_copy(
            src_ref=src, dst_ref=dst, send_sem=ss.at[j, i], recv_sem=rs.at[j, i],
            device_id=dev, device_id_type=MESH,
        )
        copy.start()
        pending.append(copy)

    def arrived(j, i, here, dev):
        pltpu.make_async_remote_copy(
            src_ref=here, dst_ref=here, send_sem=ss.at[j, i], recv_sem=rs.at[j, i],
            device_id=dev, device_id_type=MESH,
        ).wait_recv()

    own = {}
    for j in range(CHUNKS):
        for s, source in ((BWD, cot), (FWD, tok)):
            own[j, s] = pltpu.make_async_copy(
                source.at[pl.ds(j * piece, piece)], every[s].at[rows_of(j, k, y, xh, 1)], ls.at[2 * j + s]
            )
            own[j, s].start()
    load_dn = pltpu.make_async_copy(wdn, wd, ls.at[2 * CHUNKS])
    load_up = pltpu.make_async_copy(wup, wu, ls.at[2 * CHUNKS + 1])
    load_dn.start()
    load_up.start()

    barrier = pltpu.get_barrier_semaphore()
    for dev in [x_dev, xh_dev, core_dev] + z_dev + y_dev:
        pl.semaphore_signal(barrier, inc=1, device_id=dev, device_id_type=MESH)
    pl.semaphore_wait(barrier, 9)

    def ag_x(j, s):
        own[j, s].wait()
        at = every[s].at[rows_of(j, k, y, xh, 1)]
        send(j, AG_XH[s], at, at, xh_dev)

    def ag_y(j, s):
        arrived(j, AG_XH[s], every[s].at[rows_of(j, k, y, 1 - xh, 1)], xh_dev)
        at = every[s].at[rows_of(j, k, y, 0, 2)]
        for d in range(3):
            send(j, AG_Y[s] + d, at, at, y_dev[d])

    def ag_core(j, s):
        for d in range(3):
            arrived(j, AG_Y[s] + d, every[s].at[rows_of(j, k, y_from[d], 0, 2)], y_dev[d])
        at = every[s].at[rows_of(j, k, 0, 0, 8)]
        send(j, AG_CORE[s], at, at, core_dev)

    def up(j, s):
        arrived(j, AG_CORE[s], every[s].at[rows_of(j, 1 - k, 0, 0, 8)], core_dev)
        rows = pl.ds(j * chunk, chunk)

        @pl.loop(0, width // WIDE)
        def _(n):
            if s == FWD:
                value, place = dot_nn(tall[rows, :], wu[:, tile_at(n, WIDE)]), pa
            else:
                value, place = dot_nt(call[rows, :], wd[tile_at(n, WIDE), :]), pb
            place[j, :, :, :, tile_at(n, WIDE)] = value.astype(BF16).reshape(2, 4, chunk // 8, WIDE)

        if s == FWD:
            send(j, A_X, pa.at[j, 1 - xl], ra.at[j], x_dev)
        else:
            for d in range(3):
                send(j, A_Z + d, pb.at[j, :, z_to[d]], rb.at[j, d], z_dev[d])

    def sum_a(j):
        arrived(j, A_X, ra.at[j], x_dev)

        @pl.loop(0, 4)
        def _(v):
            pa[j, xl, v] = (pa[j, xl, v].astype(F32) + ra[j, v].astype(F32)).astype(BF16)

        for d in range(3):
            send(j, B_Z + d, pa.at[j, xl, z_to[d]], r3a.at[j, d], z_dev[d])
        for d in range(3):
            arrived(j, A_Z + d, rb.at[j, d], z_dev[d])

        def total(v):
            value = pb[j, v, z].astype(F32)
            for d in range(3):
                value = value + rb[j, d, v].astype(F32)
            return value

        sb[j] = total(1 - xl).astype(BF16)
        send(j, B_X, sb.at[j], r3b.at[j], x_dev)
        sbo[j] = total(xl)

    def sum_b(j):
        for d in range(3):
            arrived(j, B_Z + d, r3a.at[j, d], z_dev[d])
        arrived(j, B_X, r3b.at[j], x_dev)
        pre = pa[j, xl, z].astype(F32)
        for d in range(3):
            pre = pre + r3a[j, d].astype(F32)
        back = sbo[j] + r3b[j].astype(F32)
        root = 0.7978845608028654
        square = pre * pre
        bend = jnp.tanh(root * (pre + 0.044715 * (square * pre)))
        half = 0.5 * (1.0 + bend)
        slope = half + 0.5 * pre * (1.0 - bend * bend) * (root * (1.0 + 3 * 0.044715 * square))
        hid[j, xl, z] = (pre * half).astype(BF16)
        gra[j, xl, z] = (back * slope).astype(BF16)
        for d in range(3):
            send(j, C_Z + d, gra.at[j, xl, z], gra.at[j, xl, z], z_dev[d])
        send(j, C_X, hid.at[j, xl, z], hid.at[j, xl, z], x_dev)

    def spread(j):
        arrived(j, C_X, hid.at[j, 1 - xl, z], x_dev)
        for d in range(3):
            send(j, D_Z + d, hid.at[j, :, z], hid.at[j, :, z], z_dev[d])
        for d in range(3):
            arrived(j, C_Z + d, gra.at[j, xl, z_from[d]], z_dev[d])
        send(j, D_X, gra.at[j, xl], gra.at[j, xl], x_dev)

    def down(j, s):
        if s == FWD:
            for d in range(3):
                arrived(j, D_Z + d, hid.at[j, :, z_from[d]], z_dev[d])
        else:
            arrived(j, D_X, gra.at[j, 1 - xl], x_dev)

        @pl.loop(0, width // WIDE)
        def _(n):
            if s == FWD:
                value = dot_nn(hid[j].reshape(chunk, width), wd[:, tile_at(n, WIDE)])
            else:
                value = dot_nt(gra[j].reshape(chunk, width), wu[tile_at(n, WIDE), :])
            out[s][j, :, :, :, tile_at(n, WIDE)] = value.astype(BF16).reshape(2, 4, 2 * piece, WIDE)

        send(j, R_CORE[s], out[s].at[j, 1 - k], r_core[s].at[j], core_dev)

    def rs_core(j, s):
        arrived(j, R_CORE[s], r_core[s].at[j], core_dev)

        @pl.loop(0, 4)
        def _(v):
            out[s][j, k, v] = (out[s][j, k, v].astype(F32) + r_core[s][j, v].astype(F32)).astype(BF16)

        for d in range(3):
            send(j, R_Y[s] + d, out[s].at[j, k, y_to[d]], r_y[s].at[j, d], y_dev[d])

    def rs_y(j, s):
        for d in range(3):
            arrived(j, R_Y[s] + d, r_y[s].at[j, d], y_dev[d])
        value = out[s][j, k, y].astype(F32)
        for d in range(3):
            value = value + r_y[s][j, d].astype(F32)
        s_x[s][j] = value.astype(BF16).reshape(2, piece, width)
        send(j, R_XH[s], s_x[s].at[j, 1 - xh], r_x[s].at[j], xh_dev)

    def rs_x(j, s):
        arrived(j, R_XH[s], r_x[s].at[j], xh_dev)
        value = (s_x[s][j, xh].astype(F32) + r_x[s][j].astype(F32)).astype(BF16)
        here = pl.ds(j * piece, piece)
        if s == FWD:
            for head in range(width // HEAD_DIM):
                oh[head, here, :] = value[:, head * HEAD_DIM:(head + 1) * HEAD_DIM]
        else:
            gt[here, :] = value

    def turn(j, s):
        at = pl.ds(j * chunk, chunk)

        @pl.loop(0, tiles)
        def _(n):
            if s == FWD:
                hturn[tile_at(n), at] = hid[j, :, :, :, tile_at(n)].reshape(chunk, TILE).T
            else:
                tturn[tile_at(n), at] = tall[at, tile_at(n)].T

    stores = []

    def grad_slices(s, first, last):
        left, right, mask, place, result = (
            (hturn, call, m2d, wd, gd) if s == FWD else (tturn, gra, m2u, wu, gu)
        )

        def load(ref, t):
            if ref is gra:
                return ref[:, :, :, :, t].reshape(tokens, GRAD_WIDE)
            return ref[:, t]

        @pl.loop(first, last)
        def _(m):
            @pl.loop(0, width // GRAD_WIDE)
            def _(n):
                value = dot_nn(left[tile_at(m), :], load(right, tile_at(n, GRAD_WIDE))) * grad_scale
                for b in range(TILE // BLOCK):
                    keep = mask[pl.ds(m * (TILE // BLOCK) + b, 1), tile_at(n, GRAD_WIDE)]
                    part = value[b * BLOCK:(b + 1) * BLOCK] * keep
                    at = pl.ds(pl.multiple_of(m * TILE + b * BLOCK, BLOCK), BLOCK)
                    place[at, tile_at(n, GRAD_WIDE)] = part.astype(BF16)

        rows = pl.ds(first * TILE, (last - first) * TILE)
        copy = pltpu.make_async_copy(place.at[rows], result.at[rows], ls.at[2 * CHUNKS + 2 + len(stores)])
        copy.start()
        stores.append(copy)

    def keep_weights(mask, wide, weight, load):
        blocks = width // BLOCK
        at = lax.broadcasted_iota(jnp.int32, (blocks, width), 1)
        first = lax.broadcasted_iota(jnp.int32, (blocks, width), 0) * BLOCK
        repeat = jnp.where((at >= first) & (at < first + BLOCK), 1.0, 0.0).astype(F32)
        wide[...] = dot_nn(mask[...].astype(F32), repeat)
        load.wait()

        @pl.loop(0, blocks)
        def _(b):
            rows = pl.ds(pl.multiple_of(b * BLOCK, BLOCK), BLOCK)
            weight[rows, :] = weight[rows, :] * wide[pl.ds(b, 1), :].astype(BF16)

    both = (BWD, FWD)
    for j in range(CHUNKS):
        for s in both:
            ag_x(j, s)
    for s in both:
        ag_y(0, s)
    keep_weights(mdn, m2d, wd, load_dn)
    for s in both:
        ag_y(1, s)
    keep_weights(mup, m2u, wu, load_up)
    for j in (2, 3):
        for s in both:
            ag_y(j, s)

    def enter(j):
        for s in both:
            ag_core(j, s)
            up(j, s)

    def leave(step, j):
        for s in (FWD, BWD):
            step(j, s)

    enter(0)
    enter(1)
    sum_a(0)
    enter(2)
    sum_a(1)
    turn(0, BWD)
    sum_b(0)
    enter(3)
    turn(1, BWD)
    sum_b(1)
    spread(0)
    turn(2, BWD)
    sum_a(2)
    spread(1)
    sum_a(3)
    turn(3, BWD)
    leave(down, 0)
    sum_b(2)
    leave(rs_core, 0)
    leave(down, 1)
    sum_b(3)
    leave(rs_core, 1)
    turn(0, FWD)
    spread(2)
    turn(1, FWD)
    spread(3)
    leave(rs_y, 0)
    leave(rs_x, 0)
    leave(rs_y, 1)
    down(2, FWD)
    down(2, BWD)
    turn(2, FWD)
    leave(rs_core, 2)
    leave(rs_x, 1)
    down(3, FWD)
    down(3, BWD)
    rs_core(3, FWD)
    turn(3, FWD)
    rs_core(3, BWD)
    grad_slices(FWD, 0, 3)
    leave(rs_y, 2)
    grad_slices(FWD, 3, 6)
    rs_y(3, FWD)
    grad_slices(BWD, 0, 3)
    rs_y(3, BWD)
    grad_slices(BWD, 3, 6)
    leave(rs_x, 2)
    leave(rs_x, 3)
    for copy in pending:
        copy.wait_send()
    for copy in stores:
        copy.wait()


def hand_over(*refs):
    sources, results, held, sems = refs[:4], refs[4:8], refs[8:12], refs[12]
    moves = []
    for source, result, place in zip(sources, results, held):
        count = place.shape[0] // TILE if place.shape[0] > TILE else 1
        step = place.shape[0] // count
        for n in range(count):
            at = pl.ds(n * step, step)
            i = len(moves)
            moves.append((
                pltpu.make_async_copy(source.at[at], place.at[at], sems.at[0, i]),
                pltpu.make_async_copy(place.at[at], result.at[at], sems.at[1, i]),
            ))
    for first, _ in moves:
        first.start()
    for first, second in moves:
        first.wait()
        second.start()
    for _, second in moves:
        second.wait()


def body(tokens, up_weight, up_mask, down_weight, down_mask, grad_out):
    share, width = tokens.shape
    total = share * lax.axis_size("col")
    part = total // CHUNKS // 8
    piece = share // CHUNKS
    blocks = width // BLOCK
    c = CHUNKS
    hbm = pl.BlockSpec(memory_space=pl.ANY)
    vmem = pl.BlockSpec(memory_space=pltpu.VMEM)
    results = (
        jax.ShapeDtypeStruct((width // HEAD_DIM, share, HEAD_DIM), BF16),
        jax.ShapeDtypeStruct((share, width), BF16),
        jax.ShapeDtypeStruct(up_weight.shape, BF16),
        jax.ShapeDtypeStruct(down_weight.shape, BF16),
    )
    made = pl.pallas_call(
        kernel,
        out_shape=results,
        in_specs=[hbm, hbm, vmem, hbm, vmem, hbm],
        out_specs=(vmem, vmem, hbm, hbm),
        scratch_shapes=[
            pltpu.VMEM((total, width), BF16),
            pltpu.VMEM((total, width), BF16),
            pltpu.VMEM((width, total), BF16),
            pltpu.VMEM((width, total), BF16),
            pltpu.VMEM(up_weight.shape, BF16),
            pltpu.VMEM(down_weight.shape, BF16),
            pltpu.VMEM((blocks, width), F32),
            pltpu.VMEM((blocks, width), F32),
            pltpu.VMEM((c, 2, 4, part, width), BF16),
            pltpu.VMEM((c, 2, 4, part, width), BF16),
            pltpu.VMEM((c, 4, part, width), BF16),
            pltpu.VMEM((c, 3, 2, part, width), BF16),
            pltpu.VMEM((c, part, width), BF16),
            pltpu.VMEM((c, part, width), F32),
            pltpu.VMEM((c, 3, part, width), BF16),
            pltpu.VMEM((c, part, width), BF16),
            pltpu.VMEM((c, 2, 4, part, width), BF16),
            pltpu.VMEM((c, 2, 4, part, width), BF16),
            pltpu.VMEM((c, 2, 4, 2 * piece, width), BF16),
            pltpu.VMEM((c, 2, 4, 2 * piece, width), BF16),
            pltpu.VMEM((c, 4, 2 * piece, width), BF16),
            pltpu.VMEM((c, 4, 2 * piece, width), BF16),
            pltpu.VMEM((c, 3, 2 * piece, width), BF16),
            pltpu.VMEM((c, 3, 2 * piece, width), BF16),
            pltpu.VMEM((c, 2, piece, width), BF16),
            pltpu.VMEM((c, 2, piece, width), BF16),
            pltpu.VMEM((c, piece, width), BF16),
            pltpu.VMEM((c, piece, width), BF16),
            pltpu.SemaphoreType.DMA((c, MESSAGES)),
            pltpu.SemaphoreType.DMA((c, MESSAGES)),
            pltpu.SemaphoreType.DMA((2 * c + 8,)),
        ],
        compiler_params=pltpu.CompilerParams(
            collective_id=0, has_side_effects=True, vmem_limit_bytes=67043328
        ),
        name="layer",
    )(tokens, up_weight, up_mask, down_weight, down_mask, grad_out)
    return tuple(
        pl.pallas_call(
            hand_over,
            out_shape=results,
            in_specs=[hbm] * 4,
            out_specs=(hbm,) * 4,
            scratch_shapes=[pltpu.VMEM(r.shape, BF16) for r in results]
            + [pltpu.SemaphoreType.DMA((2, 16))],
            compiler_params=pltpu.CompilerParams(vmem_limit_bytes=67043328),
            name="hand_over",
        )(*made)
    )


def solution(mesh):
    return jax.shard_map(
        body,
        mesh=mesh,
        in_specs=(
            P("col", "row"),
            P("row", "col"),
            P("row", "col"),
            P("col", "row"),
            P("col", "row"),
            P("col", "row"),
        ),
        out_specs=(P("row", "col", None), P("col", "row"), P("row", "col"), P("col", "row")),
        check_vma=False,
    )
```

time: 190 us -> 167 us (0.88)
  Pallas kernels: 178 us -> 166 us
  local copies, waits for them, and re-layouts: 10.5 us -> 0 us
    pallas_call x1 -> x2, Pallas kernels: 178 us -> 166 us  [the longest x1 159 us: body(): pl.pallas_call(kernel, out_shape=results, in_specs=[hbm, hbm, vmem, hbm,...]
    unnamed x8 -> x0, local copies, waits for them, and re-layouts: 10.5 us -> none
where the time goes in v2:
time: 167 us
  Pallas kernels  166 us (99%)
    pallas_call x1, Pallas kernels, body(): pl.pallas_call(kernel, out_shape=results, in_specs=[hbm, hbm, vmem, hbm,...  159 us
    pallas_call x1, Pallas kernels, body(): pl.pallas_call(hand_over, out_shape=results, in_specs=[hbm] * 4, out_spec...  7.91 us

profile of v2, /device:TPU:1, one launch (start us, length us, event | category | flops | bytes accessed | tf_op | source)
XLA Modules:
  0.0 167.1 jit_solution(4026613920976829249)
XLA Ops:
  0.6 158.6 %layer.1 = (bf16[12,64,128]{2,1,0:T(8,128)(2,1)}, bf16[64,1536]{1,0:T(8,128)(2,1)}, bf16[1536,1536]{1,0:T(8,128)(2,1)}, bf16[1536,1536]{1,0:T(8,128)(2,1)}) custom-call(bf16[64,1536]{1,0:T(8,128)(2,1)} %tok.1, bf16[1536,1536]{1,0:T(8,128)(2,1)} %wup.1, s32[24,24]{1,0:T(8,128)} %mup.1, bf16[1536,1536]{1,0:T(8,128)(2,1)} %wdn.1, s32[24,24]{1,0:T(8,128)} %mdn.1, ...), custom_call_target="tpu_custom_call" | custom-call | tf_op jit(solution)/shard_map/layer/pallas_call | solution.py:404
  159.2 7.9 %hand_over.1 = (bf16[12,64,128]{2,1,0:T(8,128)(2,1)}, bf16[64,1536]{1,0:T(8,128)(2,1)}, bf16[1536,1536]{1,0:T(8,128)(2,1)}, bf16[1536,1536]{1,0:T(8,128)(2,1)}) custom-call(bf16[12,64,128]{2,1,0:T(8,128)(2,1)} %get-tuple-element.8.refs_0_, bf16[64,1536]{1,0:T(8,128)(2,1)} %get-tuple-element.9.refs_1_, bf16[1536,1536]{1,0:T(8,128)(2,1)} %get-tuple-element.10.refs_2_, ...), custom_call_target="tpu_custom_call" | custom-call | tf_op jit(solution)/shard_map/hand_over/pallas_call | solution.py:448

commit v3 on v2

--- a/solution.py
+++ b/solution.py
@@ -22,7 +22,8 @@
 R_CORE, R_Y, R_XH = (10, 15), (11, 16), (14, 19)
 A_X, A_Z, B_Z, B_X = 20, 21, 24, 27
 C_X, C_Z, D_Z, D_X = 28, 29, 32, 35
-MESSAGES = 36
+AG_Y2 = (36, 39)
+MESSAGES = 42
 FWD, BWD = 0, 1
 
 
@@ -42,7 +43,7 @@
     tok, wup, mup, wdn, mdn, cot,
     oh, gt, gu, gd,
     tall, call, tturn, hturn, wu, wd, m2u, m2d, pa, pb, ra, rb, sb, sbo, r3a, r3b, hid, gra,
-    outf, outb, r7f, r7b, ryf, ryb, s8f, s8b, rxf, rxb,
+    r7f, r7b, ryf, ryb, s8f, s8b, rxf, rxb,
     ss, rs, ls,
 ):
     width = tok.shape[1]
@@ -52,7 +53,7 @@
     tiles = width // TILE
     grad_scale = 1.0 / math.sqrt(tokens)
     every = (tall, call)
-    out, r_core, r_y, s_x, r_x = (outf, outb), (r7f, r7b), (ryf, ryb), (s8f, s8b), (rxf, rxb)
+    out, r_core, r_y, s_x, r_x = (pa, pb), (r7f, r7b), (ryf, ryb), (s8f, s8b), (rxf, rxb)
 
     row, col = lax.axis_index("row"), lax.axis_index("col")
     xl, z = row // 4, row % 4
@@ -73,7 +74,7 @@
         at = j * chunk + k_ * (chunk // 2) + y_ * (2 * piece) + xh_ * piece
         return pl.ds(pl.multiple_of(at, piece), pieces * piece)
 
-    pending = []
+    pending = {}
 
     def send(j, i, src, dst, dev):
         copy = pltpu.make_async_remote_copy(
@@ -81,7 +82,7 @@
             device_id=dev, device_id_type=MESH,
         )
         copy.start()
-        pending.append(copy)
+        pending[j, i] = copy
 
     def arrived(j, i, here, dev):
         pltpu.make_async_remote_copy(
@@ -111,15 +112,22 @@
         at = every[s].at[rows_of(j, k, y, xh, 1)]
         send(j, AG_XH[s], at, at, xh_dev)
 
+    def ag_own(j, s):
+        at = every[s].at[rows_of(j, k, y, xh, 1)]
+        for d in range(3):
+            send(j, AG_Y[s] + d, at, at, y_dev[d])
+
     def ag_y(j, s):
-        arrived(j, AG_XH[s], every[s].at[rows_of(j, k, y, 1 - xh, 1)], xh_dev)
-        at = every[s].at[rows_of(j, k, y, 0, 2)]
-        for d in range(3):
-            send(j, AG_Y[s] + d, at, at, y_dev[d])
+        at = every[s].at[rows_of(j, k, y, 1 - xh, 1)]
+        arrived(j, AG_XH[s], at, xh_dev)
+        for d in range(3):
+            send(j, AG_Y2[s] + d, at, at, y_dev[d])
 
     def ag_core(j, s):
         for d in range(3):
-            arrived(j, AG_Y[s] + d, every[s].at[rows_of(j, k, y_from[d], 0, 2)], y_dev[d])
+            arrived(j, AG_Y[s] + d, every[s].at[rows_of(j, k, y_from[d], xh, 1)], y_dev[d])
+        for d in range(3):
+            arrived(j, AG_Y2[s] + d, every[s].at[rows_of(j, k, y_from[d], 1 - xh, 1)], y_dev[d])
         at = every[s].at[rows_of(j, k, 0, 0, 8)]
         send(j, AG_CORE[s], at, at, core_dev)
 
@@ -196,6 +204,8 @@
                 arrived(j, D_Z + d, hid.at[j, :, z_from[d]], z_dev[d])
         else:
             arrived(j, D_X, gra.at[j, 1 - xl], x_dev)
+        for i in (A_X, B_Z, B_Z + 1, B_Z + 2) if s == FWD else (A_Z, A_Z + 1, A_Z + 2):
+            pending.pop((j, i)).wait_send()
 
         @pl.loop(0, width // WIDE)
         def _(n):
@@ -246,11 +256,10 @@
             else:
                 tturn[tile_at(n), at] = tall[at, tile_at(n)].T
 
-    stores = []
 
     def grad_slices(s, first, last):
-        left, right, mask, place, result = (
-            (hturn, call, m2d, wd, gd) if s == FWD else (tturn, gra, m2u, wu, gu)
+        left, right, mask, place = (
+            (hturn, call, m2d, gd) if s == FWD else (tturn, gra, m2u, gu)
         )
 
         def load(ref, t):
@@ -269,10 +278,6 @@
                     at = pl.ds(pl.multiple_of(m * TILE + b * BLOCK, BLOCK), BLOCK)
                     place[at, tile_at(n, GRAD_WIDE)] = part.astype(BF16)
 
-        rows = pl.ds(first * TILE, (last - first) * TILE)
-        copy = pltpu.make_async_copy(place.at[rows], result.at[rows], ls.at[2 * CHUNKS + 2 + len(stores)])
-        copy.start()
-        stores.append(copy)
 
     def keep_weights(mask, wide, weight, load):
         blocks = width // BLOCK
@@ -288,17 +293,22 @@
             weight[rows, :] = weight[rows, :] * wide[pl.ds(b, 1), :].astype(BF16)
 
     both = (BWD, FWD)
-    for j in range(CHUNKS):
+    for s in both:
+        ag_x(0, s)
+        ag_own(0, s)
+    for j in range(1, CHUNKS):
         for s in both:
             ag_x(j, s)
     for s in both:
         ag_y(0, s)
     keep_weights(mdn, m2d, wd, load_dn)
     for s in both:
+        ag_own(1, s)
         ag_y(1, s)
     keep_weights(mup, m2u, wu, load_up)
     for j in (2, 3):
         for s in both:
+            ag_own(j, s)
             ag_y(j, s)
 
     def enter(j):
@@ -324,25 +334,25 @@
     turn(2, BWD)
     sum_a(2)
     spread(1)
-    sum_a(3)
     turn(3, BWD)
     leave(down, 0)
     sum_b(2)
+    sum_a(3)
     leave(rs_core, 0)
     leave(down, 1)
+    spread(2)
+    leave(rs_core, 1)
     sum_b(3)
-    leave(rs_core, 1)
     turn(0, FWD)
-    spread(2)
     turn(1, FWD)
-    spread(3)
     leave(rs_y, 0)
     leave(rs_x, 0)
-    leave(rs_y, 1)
+    spread(3)
     down(2, FWD)
     down(2, BWD)
+    leave(rs_core, 2)
     turn(2, FWD)
-    leave(rs_core, 2)
+    leave(rs_y, 1)
     leave(rs_x, 1)
     down(3, FWD)
     down(3, BWD)
@@ -353,37 +363,26 @@
     leave(rs_y, 2)
     grad_slices(FWD, 3, 6)
     rs_y(3, FWD)
-    grad_slices(BWD, 0, 3)
+    grad_slices(BWD, 0, 2)
     rs_y(3, BWD)
-    grad_slices(BWD, 3, 6)
+    grad_slices(BWD, 2, 5)
     leave(rs_x, 2)
     leave(rs_x, 3)
-    for copy in pending:
+    grad_slices(BWD, 5, 6)
+    for copy in pending.values():
         copy.wait_send()
-    for copy in stores:
+
+
+def hand_over(*refs):
+    made, results, sems = refs[:4], refs[4:8], refs[8]
+    copies = [
+        pltpu.make_async_copy(source, result, sems.at[i])
+        for i, (source, result) in enumerate(zip(made, results))
+    ]
+    for copy in copies:
+        copy.start()
+    for copy in copies:
         copy.wait()
-
-
-def hand_over(*refs):
-    sources, results, held, sems = refs[:4], refs[4:8], refs[8:12], refs[12]
-    moves = []
-    for source, result, place in zip(sources, results, held):
-        count = place.shape[0] // TILE if place.shape[0] > TILE else 1
-        step = place.shape[0] // count
-        for n in range(count):
-            at = pl.ds(n * step, step)
-            i = len(moves)
-            moves.append((
-                pltpu.make_async_copy(source.at[at], place.at[at], sems.at[0, i]),
-                pltpu.make_async_copy(place.at[at], result.at[at], sems.at[1, i]),
-            ))
-    for first, _ in moves:
-        first.start()
-    for first, second in moves:
-        first.wait()
-        second.start()
-    for _, second in moves:
-        second.wait()
 
 
 def body(tokens, up_weight, up_mask, down_weight, down_mask, grad_out):
@@ -403,9 +402,9 @@
     )
     made = pl.pallas_call(
         kernel,
-        out_shape=results,
+        out_shape=tuple(pltpu.VMEM(r.shape, BF16) for r in results),
         in_specs=[hbm, hbm, vmem, hbm, vmem, hbm],
-        out_specs=(vmem, vmem, hbm, hbm),
+        out_specs=(vmem,) * 4,
         scratch_shapes=[
             pltpu.VMEM((total, width), BF16),
             pltpu.VMEM((total, width), BF16),
@@ -425,8 +424,6 @@
             pltpu.VMEM((c, part, width), BF16),
             pltpu.VMEM((c, 2, 4, part, width), BF16),
             pltpu.VMEM((c, 2, 4, part, width), BF16),
-            pltpu.VMEM((c, 2, 4, 2 * piece, width), BF16),
-            pltpu.VMEM((c, 2, 4, 2 * piece, width), BF16),
             pltpu.VMEM((c, 4, 2 * piece, width), BF16),
             pltpu.VMEM((c, 4, 2 * piece, width), BF16),
             pltpu.VMEM((c, 3, 2 * piece, width), BF16),
@@ -437,10 +434,10 @@
             pltpu.VMEM((c, piece, width), BF16),
             pltpu.SemaphoreType.DMA((c, MESSAGES)),
             pltpu.SemaphoreType.DMA((c, MESSAGES)),
-            pltpu.SemaphoreType.DMA((2 * c + 8,)),
+            pltpu.SemaphoreType.DMA((2 * c + 2,)),
         ],
         compiler_params=pltpu.CompilerParams(
-            collective_id=0, has_side_effects=True, vmem_limit_bytes=67043328
+            collective_id=0, has_side_effects=True, vmem_limit_bytes=57000000
         ),
         name="layer",
     )(tokens, up_weight, up_mask, down_weight, down_mask, grad_out)
@@ -448,11 +445,10 @@
         pl.pallas_call(
             hand_over,
             out_shape=results,
-            in_specs=[hbm] * 4,
+            in_specs=[vmem] * 4,
             out_specs=(hbm,) * 4,
-            scratch_shapes=[pltpu.VMEM(r.shape, BF16) for r in results]
-            + [pltpu.SemaphoreType.DMA((2, 16))],
-            compiler_params=pltpu.CompilerParams(vmem_limit_bytes=67043328),
+            scratch_shapes=[pltpu.SemaphoreType.DMA((4,))],
+            compiler_params=pltpu.CompilerParams(vmem_limit_bytes=1 << 20),
             name="hand_over",
         )(*made)
     )

time: 167 us -> 157 us (0.940)
  Pallas kernels: 166 us -> 156 us
    pallas_call x2, Pallas kernels: 166 us -> 156 us  [the longest x1 152 us: body(): pl.pallas_call(kernel, out_shape=tuple((pltpu.VMEM(r.shape, BF16) for r i...]
where the time goes in v3:
time: 157 us
  Pallas kernels  156 us (99%)
    pallas_call x1, Pallas kernels, body(): pl.pallas_call(kernel, out_shape=tuple((pltpu.VMEM(r.shape, BF16) for r i...  152 us
    pallas_call x1, Pallas kernels, body(): pl.pallas_call(hand_over, out_shape=results, in_specs=[vmem] * 4, out_spe...  3.91 us

profile of v3, /device:TPU:1, one launch (start us, length us, event | category | flops | bytes accessed | tf_op | source)
XLA Modules:
  0.0 156.7 jit_solution(16693875136426537211)
XLA Ops:
  0.6 152.2 %layer.1 = (bf16[12,64,128]{2,1,0:T(8,128)(2,1)S(1)}, bf16[64,1536]{1,0:T(8,128)(2,1)S(1)}, bf16[1536,1536]{1,0:T(8,128)(2,1)S(1)}, bf16[1536,1536]{1,0:T(8,128)(2,1)S(1)}) custom-call(bf16[64,1536]{1,0:T(8,128)(2,1)} %tok.1, bf16[1536,1536]{1,0:T(8,128)(2,1)} %wup.1, s32[24,24]{1,0:T(8,128)} %mup.1, bf16[1536,1536]{1,0:T(8,128)(2,1)} %wdn.1, s32[24,24]{1,0:T(8,128)} %mdn.1, ...), custom_call_target="tpu_custom_call" | custom-call | tf_op jit(solution)/shard_map/layer/pallas_call | solution.py:403
  152.8 3.9 %hand_over.1 = (bf16[12,64,128]{2,1,0:T(8,128)(2,1)}, bf16[64,1536]{1,0:T(8,128)(2,1)}, bf16[1536,1536]{1,0:T(8,128)(2,1)}, bf16[1536,1536]{1,0:T(8,128)(2,1)}) custom-call(bf16[12,64,128]{2,1,0:T(8,128)(2,1)S(1)} %get-tuple-element.8.refs_0_, bf16[64,1536]{1,0:T(8,128)(2,1)S(1)} %get-tuple-element.9.refs_1_, ...), custom_call_target="tpu_custom_call" | custom-call | tf_op jit(solution)/shard_map/hand_over/pallas_call | solution.py:445

commit v4 on v3

--- a/solution.py
+++ b/solution.py
@@ -23,7 +23,8 @@
 A_X, A_Z, B_Z, B_X = 20, 21, 24, 27
 C_X, C_Z, D_Z, D_X = 28, 29, 32, 35
 AG_Y2 = (36, 39)
-MESSAGES = 42
+A_X2, A_Z2, R_CORE2 = 42, 43, (46, 47)
+MESSAGES = 48
 FWD, BWD = 0, 1
 
 
@@ -135,22 +136,39 @@
         arrived(j, AG_CORE[s], every[s].at[rows_of(j, 1 - k, 0, 0, 8)], core_dev)
         rows = pl.ds(j * chunk, chunk)
 
-        @pl.loop(0, width // WIDE)
-        def _(n):
+        def product(at):
             if s == FWD:
-                value, place = dot_nn(tall[rows, :], wu[:, tile_at(n, WIDE)]), pa
+                value, place = dot_nn(tall[rows, :], wu[:, at]), pa
             else:
-                value, place = dot_nt(call[rows, :], wd[tile_at(n, WIDE), :]), pb
-            place[j, :, :, :, tile_at(n, WIDE)] = value.astype(BF16).reshape(2, 4, chunk // 8, WIDE)
-
-        if s == FWD:
-            send(j, A_X, pa.at[j, 1 - xl], ra.at[j], x_dev)
+                value, place = dot_nt(call[rows, :], wd[at, :]), pb
+            place[j, :, :, :, at] = value.astype(BF16).reshape(2, 4, chunk // 8, WIDE)
+
+        def leave_with(at, to_x, to_z):
+            if s == FWD:
+                send(j, to_x, pa.at[j, 1 - xl, :, :, at], ra.at[j, :, :, at], x_dev)
+            else:
+                for d in range(3):
+                    send(j, to_z + d, pb.at[j, :, z_to[d], :, at], rb.at[j, d, :, :, at], z_dev[d])
+
+        if j == 0:
+            for n, (to_x, to_z) in enumerate(((A_X, A_Z), (A_X2, A_Z2))):
+                product(pl.ds(n * WIDE, WIDE))
+                leave_with(pl.ds(n * WIDE, WIDE), to_x, to_z)
         else:
-            for d in range(3):
-                send(j, A_Z + d, pb.at[j, :, z_to[d]], rb.at[j, d], z_dev[d])
+            @pl.loop(0, width // WIDE)
+            def _(n):
+                product(tile_at(n, WIDE))
+
+            leave_with(pl.ds(0, width), A_X, A_Z)
+
+    def halves(j, at_chunk, first, second):
+        if j == at_chunk:
+            return [(first, pl.ds(0, WIDE)), (second, pl.ds(WIDE, WIDE))]
+        return [(first, pl.ds(0, width))]
 
     def sum_a(j):
-        arrived(j, A_X, ra.at[j], x_dev)
+        for i, at in halves(j, 0, A_X, A_X2):
+            arrived(j, i, ra.at[j, :, :, at], x_dev)
 
         @pl.loop(0, 4)
         def _(v):
@@ -159,7 +177,8 @@
         for d in range(3):
             send(j, B_Z + d, pa.at[j, xl, z_to[d]], r3a.at[j, d], z_dev[d])
         for d in range(3):
-            arrived(j, A_Z + d, rb.at[j, d], z_dev[d])
+            for i, at in halves(j, 0, A_Z, A_Z2):
+                arrived(j, i + d, rb.at[j, d, :, :, at], z_dev[d])
 
         def total(v):
             value = pb[j, v, z].astype(F32)
@@ -204,21 +223,36 @@
                 arrived(j, D_Z + d, hid.at[j, :, z_from[d]], z_dev[d])
         else:
             arrived(j, D_X, gra.at[j, 1 - xl], x_dev)
-        for i in (A_X, B_Z, B_Z + 1, B_Z + 2) if s == FWD else (A_Z, A_Z + 1, A_Z + 2):
-            pending.pop((j, i)).wait_send()
-
-        @pl.loop(0, width // WIDE)
-        def _(n):
+        for i in (A_X, A_X2, B_Z, B_Z + 1, B_Z + 2) if s == FWD else [
+            first + d for first in (A_Z, A_Z2) for d in range(3)
+        ]:
+            if (j, i) in pending:
+                pending.pop((j, i)).wait_send()
+
+        def product(at):
             if s == FWD:
-                value = dot_nn(hid[j].reshape(chunk, width), wd[:, tile_at(n, WIDE)])
+                value = dot_nn(hid[j].reshape(chunk, width), wd[:, at])
             else:
-                value = dot_nt(gra[j].reshape(chunk, width), wu[tile_at(n, WIDE), :])
-            out[s][j, :, :, :, tile_at(n, WIDE)] = value.astype(BF16).reshape(2, 4, 2 * piece, WIDE)
-
-        send(j, R_CORE[s], out[s].at[j, 1 - k], r_core[s].at[j], core_dev)
+                value = dot_nt(gra[j].reshape(chunk, width), wu[at, :])
+            out[s][j, :, :, :, at] = value.astype(BF16).reshape(2, 4, 2 * piece, WIDE)
+
+        def leave_with(i, at):
+            send(j, i, out[s].at[j, 1 - k, :, :, at], r_core[s].at[j, :, :, at], core_dev)
+
+        if j == CHUNKS - 1:
+            for i, at in halves(j, j, R_CORE[s], R_CORE2[s]):
+                product(at)
+                leave_with(i, at)
+        else:
+            @pl.loop(0, width // WIDE)
+            def _(n):
+                product(tile_at(n, WIDE))
+
+            leave_with(R_CORE[s], pl.ds(0, width))
 
     def rs_core(j, s):
-        arrived(j, R_CORE[s], r_core[s].at[j], core_dev)
+        for i, at in halves(j, CHUNKS - 1, R_CORE[s], R_CORE2[s]):
+            arrived(j, i, r_core[s].at[j, :, :, at], core_dev)
 
         @pl.loop(0, 4)
         def _(v):

time: 157 us -> 158 us (level)
  no operation moved by 1% of the time
where the time goes in v4:
time: 158 us; the launch traced here: 157 us
  Pallas kernels  157 us (99%)
    pallas_call x1, Pallas kernels, body(): pl.pallas_call(kernel, out_shape=tuple((pltpu.VMEM(r.shape, BF16) for r i...  153 us
    pallas_call x1, Pallas kernels, body(): pl.pallas_call(hand_over, out_shape=results, in_specs=[vmem] * 4, out_spe...  3.91 us

profile of v4, /device:TPU:1, one launch (start us, length us, event | category | flops | bytes accessed | tf_op | source)
XLA Modules:
  0.0 157.4 jit_solution(8153669458296953809)
XLA Ops:
  0.6 152.7 %layer.1 = (bf16[12,64,128]{2,1,0:T(8,128)(2,1)S(1)}, bf16[64,1536]{1,0:T(8,128)(2,1)S(1)}, bf16[1536,1536]{1,0:T(8,128)(2,1)S(1)}, bf16[1536,1536]{1,0:T(8,128)(2,1)S(1)}) custom-call(bf16[64,1536]{1,0:T(8,128)(2,1)} %tok.1, bf16[1536,1536]{1,0:T(8,128)(2,1)} %wup.1, s32[24,24]{1,0:T(8,128)} %mup.1, bf16[1536,1536]{1,0:T(8,128)(2,1)} %wdn.1, s32[24,24]{1,0:T(8,128)} %mdn.1, ...), custom_call_target="tpu_custom_call" | custom-call | tf_op jit(solution)/shard_map/layer/pallas_call | solution.py:437
  153.4 3.9 %hand_over.1 = (bf16[12,64,128]{2,1,0:T(8,128)(2,1)}, bf16[64,1536]{1,0:T(8,128)(2,1)}, bf16[1536,1536]{1,0:T(8,128)(2,1)}, bf16[1536,1536]{1,0:T(8,128)(2,1)}) custom-call(bf16[12,64,128]{2,1,0:T(8,128)(2,1)S(1)} %get-tuple-element.8.refs_0_, bf16[64,1536]{1,0:T(8,128)(2,1)S(1)} %get-tuple-element.9.refs_1_, ...), custom_call_target="tpu_custom_call" | custom-call | tf_op jit(solution)/shard_map/hand_over/pallas_call | solution.py:479
